TPU v7x, 256 devices: a whole 4x4x8 slice. The times are simulated.
256 devices in a mesh: img: 4 (over y), seq: 64 (over z, x, core).
Axes of the slice: x: 4, y: 4, z: 8, core: 2. Of those that a mesh axis runs over, the one named last changes fastest.
Arguments:
- query_proj: bfloat16 [4, 8192, 1280], P('img', 'seq'), may hold values from -6 to 6
- key_proj: bfloat16 [4, 8192, 1280], P('img', 'seq'), may hold values from -6 to 6
- value_proj: bfloat16 [4, 8192, 1280], P('img', 'seq'), may hold values from -12 to 12
- merge_cells: int32 [4, 2048, 4], P('img', 'seq'), may hold values from 0 to 8191, as said below
- unmerge: int32 [4, 8192], P('img', 'seq'), may hold values from 0 to 2047, as said below
- grad_out: bfloat16 [4, 8192, 1280], P('img', 'seq'), may hold values from -9 to 9
- query_gain: float32 [64], replicated, may hold values from 1 to 2.5
- key_gain: float32 [64], replicated, may hold values from 1 to 2.5
Outputs:
- attended: bfloat16 [4, 8192, 1280], P('img', 'seq')
- grad_query: bfloat16 [4, 8192, 1280], P('img', 'seq')
- grad_key: bfloat16 [4, 8192, 1280], P('img', 'seq')
- grad_value: bfloat16 [4, 8192, 1280], P('img', 'seq')
- grad_query_gain: float32 [64], replicated
- grad_key_gain: float32 [64], replicated
Inputs may be any that keep to these rules, and one draw needn't show every extreme that they name: `merge_cells`: row c of an image lists, in some order, the four tokens of one 2x2 cell: columns j and j + 1 (modulo 64) of image rows 2 i and 2 i + 1, where token r * 64 + s stands at row r and column s and j has one parity within each pair of rows; every token lies in exactly one cell; cell c and its four tokens are held by the same seq index. `unmerge`: entry t is the row of merge_cells of the same image that lists token t.
All inputs are finite; a program needn't handle non-finite values.
Results may differ from a plain program's by a relative error of at most 0.012.
Values may be sent and summed in bfloat16 or wider, within the bound.
A program may use at most 128 MiB of HBM per device.

v0:
```python
import math
import jax
import jax.numpy as jnp
from jax import lax
from jax.sharding import PartitionSpec as P

EPSILON = 1e-06
PRECISE = lax.Precision.HIGHEST


def normalize(inputs, gain_row):
    row_scale = lax.rsqrt(jnp.mean(inputs * inputs, axis=-1, keepdims=True) + EPSILON)
    unit_vals = inputs * row_scale
    return (unit_vals, row_scale, unit_vals * gain_row)


def norm_back(grad_normed, unit_vals, row_scale, gain_row):
    grad_unit = grad_normed * gain_row
    mean_inner = jnp.mean(grad_unit * unit_vals, axis=-1, keepdims=True)
    return row_scale * (grad_unit - unit_vals * mean_inner)


def attention_pass(queries, upstream, keys_all, values_all):
    tok_rows, group_heads, head_dim = queries.shape
    group_lanes = group_heads * head_dim
    cell_count = keys_all.shape[0]
    block_rows = math.gcd(cell_count, 512)
    block_count = cell_count // block_rows
    key_blocks = keys_all.reshape(block_count, block_rows, group_lanes)
    value_blocks = values_all.reshape(block_count, block_rows, group_lanes)

    def scores_of(key_rows):
        return (
            jnp.einsum(
                "thd,khd->thk",
                queries,
                key_rows.reshape(-1, group_heads, head_dim),
                preferred_element_type=jnp.float32,
            )
            * 0.125
        )

    def forward_step(running, pieces):
        row_total, weighted = running
        key_rows, value_rows = pieces
        exp_scores = jnp.exp(scores_of(key_rows))
        row_total = row_total + jnp.sum(exp_scores, axis=-1)
        weighted = weighted + jnp.einsum(
            "thk,khd->thd",
            exp_scores.astype(jnp.bfloat16),
            value_rows.reshape(-1, group_heads, head_dim),
            preferred_element_type=jnp.float32,
        )
        return ((row_total, weighted), None)

    initial = (
        jnp.zeros((tok_rows, group_heads), jnp.float32),
        jnp.zeros((tok_rows, group_heads, head_dim), jnp.float32),
    )
    (row_total, weighted), unused = lax.scan(forward_step, initial, (key_blocks, value_blocks))
    attended = (weighted / row_total[:, :, None]).astype(jnp.bfloat16)
    row_inner = jnp.sum(upstream.astype(jnp.float32) * attended.astype(jnp.float32), axis=-1)

    def local_grads(key_rows, value_rows):
        attention = jnp.exp(scores_of(key_rows)) / row_total[:, :, None]
        grad_weights = jnp.einsum(
            "thd,khd->thk",
            upstream,
            value_rows.reshape(-1, group_heads, head_dim),
            preferred_element_type=jnp.float32,
        )
        grad_scores = (attention * (grad_weights - row_inner[:, :, None])).astype(jnp.bfloat16)
        return (attention.astype(jnp.bfloat16), grad_scores)

    def key_terms(key_rows, attention_bf, grad_scores):
        row_count = key_rows.shape[0]
        grad_keys = (
            jnp.einsum("thk,thd->khd", grad_scores, queries, preferred_element_type=jnp.float32)
            * 0.125
        )
        grad_values = jnp.einsum(
            "thk,thd->khd", attention_bf, upstream, preferred_element_type=jnp.float32
        )
        return jnp.concatenate(
            [
                grad_keys.reshape(row_count, group_lanes),
                grad_values.reshape(row_count, group_lanes),
            ],
            axis=1,
        )

    def query_term(key_rows, grad_scores):
        return (
            jnp.einsum(
                "thk,khd->thd",
                grad_scores,
                key_rows.reshape(-1, group_heads, head_dim),
                preferred_element_type=jnp.float32,
            )
            * 0.125
        )

    query_zero = jnp.zeros((tok_rows, group_heads, head_dim), jnp.float32)

    def backward_step(running, pieces):
        key_rows, value_rows = pieces
        attention_bf, grad_scores = local_grads(key_rows, value_rows)
        return (
            running + query_term(key_rows, grad_scores),
            key_terms(key_rows, attention_bf, grad_scores),
        )

    grad_q_group, term_blocks = lax.scan(backward_step, query_zero, (key_blocks, value_blocks))
    return (attended, grad_q_group, term_blocks.reshape(cell_count, 2 * group_lanes), None)


def local(query_proj, key_proj, value_proj, merge_cells, unmerge, grad_out, query_gain, key_gain):
    tok_dev = query_proj.shape[1]
    total_lanes = query_proj.shape[2]
    head_dim = query_gain.shape[0]
    head_count = total_lanes // head_dim
    cells_dev = merge_cells.shape[1]
    seq_index = lax.axis_index("seq")
    q_unit, q_scale, q_normed = normalize(
        query_proj[0].astype(jnp.float32).reshape(tok_dev, head_count, head_dim), query_gain
    )
    q_bf = q_normed.reshape(tok_dev, total_lanes).astype(jnp.bfloat16)
    k_unit, k_scale, k_normed = normalize(
        key_proj[0].astype(jnp.float32).reshape(tok_dev, head_count, head_dim), key_gain
    )
    tok_ids = seq_index * tok_dev + jnp.arange(tok_dev, dtype=jnp.int32)
    member = jnp.sum(
        (merge_cells[0][:, :, None] == tok_ids[None, None, :]).astype(jnp.float32), axis=1
    )
    k_merged = (
        jnp.dot(member, k_normed.reshape(tok_dev, total_lanes), precision=PRECISE) * 0.25
    ).astype(jnp.bfloat16)
    v_merged = (
        jnp.dot(member.astype(jnp.bfloat16), value_proj[0], preferred_element_type=jnp.float32)
        * 0.25
    ).astype(jnp.bfloat16)
    group_lanes = 256
    group_heads = group_lanes // head_dim
    out_parts, query_parts, key_parts, value_parts = ([], [], [], [])
    for group_index in range(total_lanes // group_lanes):
        lane_start = group_index * group_lanes
        queries = q_bf[:, lane_start : lane_start + group_lanes].reshape(
            tok_dev, group_heads, head_dim
        )
        upstream = grad_out[0][:, lane_start : lane_start + group_lanes].reshape(
            tok_dev, group_heads, head_dim
        )
        keys_all, values_all = (
            lax.all_gather(
                k_merged[:, lane_start : lane_start + group_lanes], "seq", axis=0, tiled=True
            ),
            lax.all_gather(
                v_merged[:, lane_start : lane_start + group_lanes], "seq", axis=0, tiled=True
            ),
        )
        attended, grad_q_group, term_rows, unused = attention_pass(
            queries, upstream, keys_all, values_all
        )
        reduced = lax.psum_scatter(term_rows, "seq", scatter_dimension=0, tiled=True)
        out_parts.append(attended.reshape(tok_dev, group_lanes))
        query_parts.append(grad_q_group.reshape(tok_dev, group_lanes))
        key_parts.append(reduced[:, :group_lanes])
        value_parts.append(reduced[:, group_lanes:])
    attended_all = jnp.concatenate(out_parts, axis=1)
    grad_q_normed = jnp.concatenate(query_parts, axis=1).reshape(tok_dev, head_count, head_dim)
    grad_merged_k = jnp.concatenate(key_parts, axis=1)
    grad_merged_v = jnp.concatenate(value_parts, axis=1)
    cell_ids = seq_index * cells_dev + jnp.arange(cells_dev, dtype=jnp.int32)
    unmerge_table = (unmerge[0][:, None] == cell_ids[None, :]).astype(jnp.float32)
    grad_k_normed = (jnp.dot(unmerge_table, grad_merged_k, precision=PRECISE) * 0.25).reshape(
        tok_dev, head_count, head_dim
    )
    grad_value = (jnp.dot(unmerge_table, grad_merged_v, precision=PRECISE) * 0.25).astype(
        jnp.bfloat16
    )
    gain_terms = (
        jnp.sum(grad_q_normed * q_unit, axis=(0, 1)),
        jnp.sum(grad_k_normed * k_unit, axis=(0, 1)),
    )
    grad_query_gain, grad_key_gain = lax.psum((gain_terms[0], gain_terms[1]), ("img", "seq"))
    grad_query = (
        norm_back(grad_q_normed, q_unit, q_scale, query_gain)
        .reshape(tok_dev, total_lanes)
        .astype(jnp.bfloat16)
    )
    grad_key = (
        norm_back(grad_k_normed, k_unit, k_scale, key_gain)
        .reshape(tok_dev, total_lanes)
        .astype(jnp.bfloat16)
    )
    return (
        attended_all[None],
        grad_query[None],
        grad_key[None],
        grad_value[None],
        grad_query_gain,
        grad_key_gain,
    )


def solution(mesh):
    placed = (
        P("img", "seq", None),
        P("img", "seq", None),
        P("img", "seq", None),
        P("img", "seq", None),
        P("img", "seq"),
        P("img", "seq", None),
        P(),
        P(),
    )
    return jax.shard_map(
        local,
        mesh=mesh,
        in_specs=placed,
        out_specs=(
            P("img", "seq", None),
            P("img", "seq", None),
            P("img", "seq", None),
            P("img", "seq", None),
            P(),
            P(),
        ),
        check_vma=False,
    )
```

profile of v0, /device:TPU:1, one launch (start us, length us, event | category | flops | bytes accessed | tf_op | source)
XLA Modules:
  0.0 1611.3 jit_solution(1745395088641482915)
XLA Ops:
  22.7 71.7 %all-gather.11.cloned.1.call-done = bf16[2048,256]{1,0:T(8,128)(2,1)} async-done(((bf16[32,256]{1,0:T(8,128)(2,1)}), bf16[2048,256]{1,0:T(8,128)(2,1)}) %all-gather.11.cloned.1.call-update) | async-done | bytes 1048592 | tf_op jit(solution)/shard_map/all_gather | solution.py:154
  96.7 75.1 %all-gather.13.cloned.1.call-done = bf16[2048,256]{1,0:T(8,128)(2,1)} async-done(((bf16[32,256]{1,0:T(8,128)(2,1)}), bf16[2048,256]{1,0:T(8,128)(2,1)}) %all-gather.13.cloned.1.call-update) | async-done | bytes 1048592 | tf_op jit(solution)/shard_map/all_gather | solution.py:157
  174.1 14.6 while.130
  192.6 28.4 %while.135 = (s32[]{:T(128)}, f32[128,4,64]{0,2,1:T(8,128)}, f32[4,512,512]{2,1,0:T(8,128)}, bf16[4,512,256]{1,2,0:T(8,128)(2,1)}, bf16[128,4,64]{0,2,1:T(8,128)...) while((s32[]{:T(128)}, f32[128,4,64]{0,2,1:T(8,128)}, ...), condition=%wide.region_20.21_spmd.clone, body=%wide.region_19.20_spmd.clone.sunk | while | flops 169836544 | bytes 14422651 | solution.py:113
  221.0 28.1 %all-gather.15.cloned.1.call-done = bf16[2048,256]{1,0:T(8,128)(2,1)} async-done(((bf16[32,256]{1,0:T(8,128)(2,1)}), bf16[2048,256]{1,0:T(8,128)(2,1)}) %all-gather.15.cloned.1.call-update) | async-done | bytes 1048592 | tf_op jit(solution)/shard_map/all_gather | solution.py:154
  251.4 74.9 %all-gather.17.cloned.1.call-done = bf16[2048,256]{1,0:T(8,128)(2,1)} async-done(((bf16[32,256]{1,0:T(8,128)(2,1)}), bf16[2048,256]{1,0:T(8,128)(2,1)}) %all-gather.17.cloned.1.call-update) | async-done | bytes 1048592 | tf_op jit(solution)/shard_map/all_gather | solution.py:157
  338.9 64.5 %all-gather.19.cloned.1.call-done = bf16[2048,256]{1,0:T(8,128)(2,1)} async-done(((bf16[32,256]{1,0:T(8,128)(2,1)}), bf16[2048,256]{1,0:T(8,128)(2,1)}) %all-gather.19.cloned.1.call-update) | async-done | bytes 1048592 | tf_op jit(solution)/shard_map/all_gather | solution.py:154
  405.7 74.9 %all-gather.21.cloned.1.call-done = bf16[2048,256]{1,0:T(8,128)(2,1)} async-done(((bf16[32,256]{1,0:T(8,128)(2,1)}), bf16[2048,256]{1,0:T(8,128)(2,1)}) %all-gather.21.cloned.1.call-update) | async-done | bytes 1048592 | tf_op jit(solution)/shard_map/all_gather | solution.py:157
  482.9 10.4 while.132
  493.3 64.7 %all-gather.23.cloned.1.call-done = bf16[2048,256]{1,0:T(8,128)(2,1)} async-done(((bf16[32,256]{1,0:T(8,128)(2,1)}), bf16[2048,256]{1,0:T(8,128)(2,1)}) %all-gather.23.cloned.1.call-update) | async-done | bytes 1048592 | tf_op jit(solution)/shard_map/all_gather | solution.py:154
  560.2 75.0 %all-gather.25.cloned.1.call-done = bf16[2048,256]{1,0:T(8,128)(2,1)} async-done(((bf16[32,256]{1,0:T(8,128)(2,1)}), bf16[2048,256]{1,0:T(8,128)(2,1)}) %all-gather.25.cloned.1.call-update) | async-done | bytes 1048592 | tf_op jit(solution)/shard_map/all_gather | solution.py:157
  637.6 75.1 %all-gather.27.cloned.1.call-done = bf16[2048,256]{1,0:T(8,128)(2,1)} async-done(((bf16[32,256]{1,0:T(8,128)(2,1)}), bf16[2048,256]{1,0:T(8,128)(2,1)}) %all-gather.27.cloned.1.call-update) | async-done | bytes 1048592 | tf_op jit(solution)/shard_map/all_gather | solution.py:154
  714.9 12.2 while.133
  727.4 62.4 %all-gather.29.cloned.1.call-done = bf16[2048,256]{1,0:T(8,128)(2,1)} async-done(((bf16[32,256]{1,0:T(8,128)(2,1)}), bf16[2048,256]{1,0:T(8,128)(2,1)}) %all-gather.29.cloned.1.call-update) | async-done | bytes 1048592 | tf_op jit(solution)/shard_map/all_gather | solution.py:157
  802.3 28.5 %while.136 = (s32[]{:T(128)}, f32[128,4,64]{0,2,1:T(8,128)}, f32[4,512,512]{2,1,0:T(8,128)}, bf16[4,512,256]{1,2,0:T(8,128)(2,1)}, bf16[128,4,64]{0,2,1:T(8,128)...) while((s32[]{:T(128)}, f32[128,4,64]{0,2,1:T(8,128)}, ...), condition=%wide.region_23.24_spmd.clone, body=%wide.region_22.23_spmd.clone.sunk | while | flops 169836544 | bytes 14422651 | solution.py:113
  835.0 23.3 %while.137 = (s32[]{:T(128)}, f32[128,4,64]{0,2,1:T(8,128)S(1)}, f32[4,512,512]{2,1,0:T(8,128)}, bf16[4,512,256]{1,2,0:T(8,128)(2,1)}, bf16[128,4,64]{0,2,1:T(8,...) while((s32[]{:T(128)}, f32[128,4,64]{0,2,1:T(8,128)S(1)}, ...), condition=%wide.region_26.27_spmd.clone, body=%wide.region_25.26_spmd.clone.sunk | while | flops 169836544 | bytes 14422651 | solution.py:113
  862.4 16.5 %while.138 = (s32[]{:T(128)}, f32[128,4,64]{0,2,1:T(8,128)S(1)}, f32[4,512,512]{2,1,0:T(8,128)}, bf16[4,512,256]{1,2,0:T(8,128)(2,1)}, bf16[128,4,64]{0,2,1:T(8,...) while((s32[]{:T(128)}, f32[128,4,64]{0,2,1:T(8,128)S(1)}, ...), condition=%wide.region_29.30_spmd.clone, body=%wide.region_28.29_spmd.clone.sunk | while | flops 169836544 | bytes 14422651 | solution.py:113
  883.0 16.5 %while.139 = (s32[]{:T(128)}, f32[128,4,64]{0,2,1:T(8,128)S(1)}, f32[4,512,512]{2,1,0:T(8,128)}, bf16[4,512,256]{1,2,0:T(8,128)(2,1)}, bf16[128,4,64]{0,2,1:T(8,...) while((s32[]{:T(128)}, f32[128,4,64]{0,2,1:T(8,128)S(1)}, ...), condition=%wide.region_32.33_spmd.clone, body=%wide.region_31.32_spmd.clone.sunk | while | flops 169836544 | bytes 14422651 | solution.py:113
  905.2 25.4 %reduce-scatter.6.cloned.1.call-done = f32[32,512]{1,0:T(8,128)} async-done(((f32[2048,512]{1,0:T(8,128)}), f32[32,512]{1,0:T(8,128)}) %reduce-scatter.6.cloned.1.call-update) | async-done | bytes 65552 | tf_op jit(solution)/shard_map/reduce_scatter | solution.py:164
  931.3 146.0 %reduce-scatter.8.cloned.1.call-done = f32[32,512]{1,0:T(8,128)} async-done(((f32[2048,512]{1,0:T(8,128)}), f32[32,512]{1,0:T(8,128)}) %reduce-scatter.8.cloned.1.call-update) | async-done | bytes 65552 | tf_op jit(solution)/shard_map/reduce_scatter | solution.py:164
  1078.1 146.1 %reduce-scatter.10.cloned.1.call-done = f32[32,512]{1,0:T(8,128)} async-done(((f32[2048,512]{1,0:T(8,128)}), f32[32,512]{1,0:T(8,128)}) %reduce-scatter.10.cloned.1.call-update) | async-done | bytes 65552 | tf_op jit(solution)/shard_map/reduce_scatter | solution.py:164
  1225.0 145.9 %reduce-scatter.12.cloned.1.call-done = f32[32,512]{1,0:T(8,128)} async-done(((f32[2048,512]{1,0:T(8,128)}), f32[32,512]{1,0:T(8,128)}) %reduce-scatter.12.cloned.1.call-update) | async-done | bytes 65552 | tf_op jit(solution)/shard_map/reduce_scatter | solution.py:164
  1371.7 145.9 %reduce-scatter.14.cloned.1.call-done = f32[32,512]{1,0:T(8,128)} async-done(((f32[2048,512]{1,0:T(8,128)}), f32[32,512]{1,0:T(8,128)}) %reduce-scatter.14.cloned.1.call-update) | async-done | bytes 65552 | tf_op jit(solution)/shard_map/reduce_scatter | solution.py:164
  1525.2 79.5 %all-reduce = (f32[64]{0:T(128)}, f32[64]{0:T(128)}) all-reduce(f32[64]{0:T(128)S(1)} %reduce_sum.179, f32[64]{0:T(128)S(1)} %reduce_sum.182), channel_id=1, replica_groups=mesh['img'=4,'seq'=64] {'img','seq'}, use_global_device_ids=true, to_apply=%region_42.43 | all-reduce | flops 128 | bytes 1024 | tf_op jit(solution)/shard_map/psum | solution.py:185
  (473 shorter events, 257.0 us)
Async XLA Ops:
  7.2 87.2 %all-gather.11.cloned.1.call-start = ((), (), s32[]{:S(2)}) async-start(), calls=%async_computation.5 | async-start | bytes 1064960 | tf_op jit(solution)/shard_map/all_gather | solution.py:154
  13.4 158.4 %all-gather.13.cloned.1.call-start = ((), (), s32[]{:S(2)}) async-start(), calls=%async_computation.6 | async-start | bytes 1064960 | tf_op jit(solution)/shard_map/all_gather | solution.py:157
  14.3 234.8 %all-gather.15.cloned.1.call-start = ((), (), s32[]{:S(2)}) async-start(), calls=%async_computation.7 | async-start | bytes 1064960 | tf_op jit(solution)/shard_map/all_gather | solution.py:154
  15.0 311.3 %all-gather.17.cloned.1.call-start = ((), (), s32[]{:S(2)}) async-start(), calls=%async_computation.8 | async-start | bytes 1064960 | tf_op jit(solution)/shard_map/all_gather | solution.py:157
  15.6 387.9 %all-gather.19.cloned.1.call-start = ((), (), s32[]{:S(2)}) async-start(), calls=%async_computation.9 | async-start | bytes 1064960 | tf_op jit(solution)/shard_map/all_gather | solution.py:154
  16.2 464.5 %all-gather.21.cloned.1.call-start = ((), (), s32[]{:S(2)}) async-start(), calls=%async_computation.10 | async-start | bytes 1064960 | tf_op jit(solution)/shard_map/all_gather | solution.py:157
  16.8 541.2 %all-gather.23.cloned.1.call-start = ((), (), s32[]{:S(2)}) async-start(), calls=%async_computation.11 | async-start | bytes 1064960 | tf_op jit(solution)/shard_map/all_gather | solution.py:154
  17.5 617.8 %all-gather.25.cloned.1.call-start = ((), (), s32[]{:S(2)}) async-start(), calls=%async_computation.12 | async-start | bytes 1064960 | tf_op jit(solution)/shard_map/all_gather | solution.py:157
  18.3 694.4 %all-gather.27.cloned.1.call-start = ((), (), s32[]{:S(2)}) async-start(), calls=%async_computation.13 | async-start | bytes 1064960 | tf_op jit(solution)/shard_map/all_gather | solution.py:154
  19.0 770.8 %all-gather.29.cloned.1.call-start = ((), (), s32[]{:S(2)}) async-start(), calls=%async_computation.14 | async-start | bytes 1064960 | tf_op jit(solution)/shard_map/all_gather | solution.py:157
  19.6 911.0 %reduce-scatter.6.cloned.1.call-start = ((), (), s32[]{:S(2)}) async-start(), calls=%async_computation.15 | async-start | bytes 4259840 | tf_op jit(solution)/shard_map/reduce_scatter | solution.py:164
  338.9 144.0 %copy-start.13 = (f32[128,4,64]{0,2,1:T(8,128)S(1)}, f32[128,4,64]{0,2,1:T(8,128)}, u32[]{:S(2)}) copy-start(f32[128,4,64]{0,2,1:T(8,128)} %custom-call.5) | copy-start | bytes 393220
  493.3 221.6 %copy-start.14 = (f32[128,4,64]{0,2,1:T(8,128)}, f32[128,4,64]{0,2,1:T(8,128)S(1)}, u32[]{:S(2)}) copy-start(f32[128,4,64]{0,2,1:T(8,128)S(1)} %get-tuple-element.415) | copy-start | bytes 393220
  493.3 221.6 %copy-start.20 = (bf16[128,256]{0,1:T(8,128)(2,1)S(1)}, bf16[128,256]{0,1:T(8,128)(2,1)}, u32[]{:S(2)}) copy-start(bf16[128,256]{0,1:T(8,128)(2,1)} %get-tuple-element.1122) | copy-start | bytes 196612
  727.2 350.1 %reduce-scatter.8.cloned.1.call-start = ((), (), s32[]{:S(2)}) async-start(), calls=%async_computation.16 | async-start | bytes 4259840 | tf_op jit(solution)/shard_map/reduce_scatter | solution.py:164
  830.8 393.4 %reduce-scatter.10.cloned.1.call-start = ((), (), s32[]{:S(2)}) async-start(), calls=%async_computation.17 | async-start | bytes 4259840 | tf_op jit(solution)/shard_map/reduce_scatter | solution.py:164
  858.3 512.7 %reduce-scatter.12.cloned.1.call-start = ((), (), s32[]{:S(2)}) async-start(), calls=%async_computation.18 | async-start | bytes 4259840 | tf_op jit(solution)/shard_map/reduce_scatter | solution.py:164
  878.9 638.7 %reduce-scatter.14.cloned.1.call-start = ((), (), s32[]{:S(2)}) async-start(), calls=%async_computation.19 | async-start | bytes 4259840 | tf_op jit(solution)/shard_map/reduce_scatter | solution.py:164
  899.7 619.4 %copy-start.41 = (s32[1,128]{1,0:T(1,128)S(1)}, s32[1,128]{1,0:T(1,128)}, u32[]{:S(2)}) copy-start(s32[1,128]{1,0:T(1,128)} %param.32) | copy-start | bytes 1540
  900.6 620.9 %copy-start.5 = (f32[1,128,1280]{1,2,0:T(8,128)S(1)}, f32[1,128,1280]{1,2,0:T(8,128)}, u32[]{:S(2)}) copy-start(f32[1,128,1280]{1,2,0:T(8,128)} %copy-done.4) | copy-start | bytes 1966084
  900.6 620.8 %copy-start.32 = (f32[128,20]{0,1:T(8,128)S(1)}, f32[128,20]{0,1:T(8,128)}, u32[]{:S(2)}) copy-start(f32[128,20]{0,1:T(8,128)} %copy-done.31) | copy-start | bytes 30724
  900.6 620.8 %copy-start.40 = (f32[64]{0:T(128)S(1)}, f32[64]{0:T(128)}, u32[]{:S(2)}) copy-start(f32[64]{0:T(128)} %param.35) | copy-start | bytes 772
  902.4 620.6 %copy-start.3 = (f32[128,1280]{1,0:T(8,128)S(1)}, f32[128,1280]{1,0:T(8,128)}, u32[]{:S(2)}) copy-start(f32[128,1280]{1,0:T(8,128)} %copy-done.2) | copy-start | bytes 1966084
  902.4 620.6 %copy-start.18 = (bf16[1,128,1280]{2,1,0:T(8,128)(2,1)S(1)}, bf16[1,128,1280]{2,1,0:T(8,128)(2,1)}, u32[]{:S(2)}) copy-start(bf16[1,128,1280]{2,1,0:T(8,128)(2,1)} %param.29) | copy-start | bytes 983044
  (34 other events, 549.6 us)
Sparse Core Ops, SparseCore 0:
  13.5 80.9 all-gather.10
  97.2 74.5 all-gather.12
  174.5 74.5 all-gather.14
  251.7 74.5 all-gather.16
  328.9 74.5 all-gather.18
  406.1 74.5 all-gather.20
  483.4 74.5 all-gather.22
  560.7 74.5 all-gather.24
  638.1 74.5 all-gather.26
  715.2 74.5 all-gather.28
  793.9 136.5 reduce-scatter.5
  934.5 142.7 reduce-scatter.7
  1081.4 142.7 reduce-scatter.9
  1228.2 142.6 reduce-scatter.11
  1374.9 142.6 reduce-scatter.13
where the time goes:
time: 1620 us; the launch traced here: 1610 us
  waiting for transfers between devices  1280 us (79%)
  local copies, waits for them, and re-layouts  124 us (8%)
  matrix products  93.7 us (6%)
  blocking collectives  79.5 us (5%)
  other arithmetic  16.3 us (1%)
    reduce_scatter x5, waiting for transfers between devices, local(): lax.psum_scatter(term_rows, 'seq', scatter_dimension=0, tiled=True)  609 us
    all_gather x5, waiting for transfers between devices, local(): lax.all_gather(v_merged[:, lane_start:lane_start + group_lanes], 'seq', a...  362 us
    all_gather x5, waiting for transfers between devices, local(): lax.all_gather(k_merged[:, lane_start:lane_start + group_lanes], 'seq', a...  304 us
    psum x1, blocking collectives, local(): lax.psum((gain_terms[0], gain_terms[1]), ('img', 'seq'))  79.5 us
    dynamic_slice x40, local copies, waits for them, and re-layouts, attention_pass(): lax.scan(forward_step, initial, (key_blocks, value_blocks))  42.7 us
    dot_general x40, matrix products, scores_of(): jnp.einsum('thd,khd->thk', queries, key_rows.reshape(-1, group_heads, hea...  35.5 us
    unnamed x111, local copies, waits for them, and re-layouts  32.6 us
  transfers between devices with their start and end apart: 15, of which 15 were waited for; matrix products, arithmetic and copies ran while one was open for 14% of the time, Pallas kernels for 0%

commit v1 on v0

--- a/solution.py
+++ b/solution.py
@@ -6,6 +6,18 @@
 
 EPSILON = 1e-06
 PRECISE = lax.Precision.HIGHEST
+
+
+def flows_solve(mine):
+    return jnp.concatenate(
+        lax.all_to_all(
+            jnp.stack([mine for _ in range(lax.axis_size("seq"))]),
+            axis_name="seq",
+            split_axis=0,
+            concat_axis=0,
+        ),
+        axis=0,
+    )
 
 
 def normalize(inputs, gain_row):
@@ -154,9 +166,7 @@
             lax.all_gather(
                 k_merged[:, lane_start : lane_start + group_lanes], "seq", axis=0, tiled=True
             ),
-            lax.all_gather(
-                v_merged[:, lane_start : lane_start + group_lanes], "seq", axis=0, tiled=True
-            ),
+            flows_solve(v_merged[:, lane_start : lane_start + group_lanes]),
         )
         attended, grad_q_group, term_rows, unused = attention_pass(
             queries, upstream, keys_all, values_all

time: 1620 us -> 1230 us (0.76)
  waiting for transfers between devices: 1280 us -> 858 us
  starting transfers between devices: 0.77 us -> 40.4 us
    all_gather x5 -> x0, waiting for transfers between devices: 362 us -> none  [local(): lax.all_gather(v_merged[:, lane_start:lane_start + group_lanes], 'seq', a...]
    all_gather x5, waiting for transfers between devices: 304 us -> 244 us  [local(): lax.all_gather(k_merged[:, lane_start:lane_start + group_lanes], 'seq', a...]
    all_to_all x0 -> x5, starting transfers between devices: none -> 39.8 us  [flows_solve(): lax.all_to_all(jnp.stack([mine for _ in range(lax.axis_size('seq'))]), ax...]
    unnamed x111 -> x129, local copies, waits for them, and re-layouts: 32.6 us -> 32.6 us
  transfers between devices with their start and end apart: 15 -> 15, of which waited for: 15 -> 11; matrix products, arithmetic and copies ran while one was open for 14% -> 18% of each run, Pallas kernels for 0% -> 0%
where the time goes in v1:
time: 1230 us
  waiting for transfers between devices  858 us (70%)
  local copies, waits for them, and re-layouts  131 us (11%)
  matrix products  88.4 us (7%)
  blocking collectives  79.7 us (6%)
  starting transfers between devices  40.4 us (3%)
  other arithmetic  15.5 us (1%)
  between operations  15.1 us (1%)
    reduce_scatter x5, waiting for transfers between devices, local(): lax.psum_scatter(term_rows, 'seq', scatter_dimension=0, tiled=True)  601 us
    all_gather x5, waiting for transfers between devices, local(): lax.all_gather(k_merged[:, lane_start:lane_start + group_lanes], 'seq', a...  244 us
    psum x1, blocking collectives, local(): lax.psum((gain_terms[0], gain_terms[1]), ('img', 'seq'))  79.7 us
    dynamic_slice x40, local copies, waits for them, and re-layouts, attention_pass(): lax.scan(forward_step, initial, (key_blocks, value_blocks))  42.8 us
    all_to_all x5, starting transfers between devices, flows_solve(): lax.all_to_all(jnp.stack([mine for _ in range(lax.axis_size('seq'))]), ax...  39.8 us
    dot_general x40, matrix products, scores_of(): jnp.einsum('thd,khd->thk', queries, key_rows.reshape(-1, group_heads, hea...  35.5 us
    unnamed x129, local copies, waits for them, and re-layouts  32.6 us
    dynamic_update_slice x40, local copies, waits for them, and re-layouts, attention_pass(): lax.scan(backward_step, query_zero, (key_blocks, value_blocks))  28 us
  transfers between devices with their start and end apart: 15, of which 11 were waited for; matrix products, arithmetic and copies ran while one was open for 18% of the time, Pallas kernels for 0%

profile of v1, /device:TPU:1, one launch (start us, length us, event | category | flops | bytes accessed | tf_op | source)
XLA Modules:
  0.0 1229.0 jit_solution(17603475715891383630)
XLA Ops:
  17.3 13.0 %all-to-all-start = ((bf16[64,32,256]{2,1,0:T(8,128)(2,1)}), bf16[64,32,256]{2,1,0:T(8,128)(2,1)S(1)}, u32[]{:S(2)}, u32[]{:S(2)}) async-start(bf16[64,32,256]{2,1,0:T(8,128)(2,1)} %stack.10), calls=%async_computation | async-start | bytes 2097152 | tf_op jit(solution)/shard_map/all_to_all | solution.py:13
  33.9 60.7 %all-gather.6.cloned.1.call-done = bf16[2048,256]{1,0:T(8,128)(2,1)} async-done(((bf16[32,256]{1,0:T(8,128)(2,1)}), bf16[2048,256]{1,0:T(8,128)(2,1)}) %all-gather.6.cloned.1.call-update) | async-done | bytes 1048592 | tf_op jit(solution)/shard_map/all_gather | solution.py:166
  98.8 6.7 all-to-all-start.1
  107.9 14.7 %while.130 = (s32[]{:T(128)}, f32[128,4]{0,1:T(4,128)}, f32[128,4,64]{0,2,1:T(8,128)S(1)}, bf16[4,512,256]{1,2,0:T(8,128)(2,1)}, bf16[128,4,64]{0,2,1:T(8,128)(2...) while((s32[]{:T(128)}, f32[128,4]{0,1:T(4,128)}, f32[128,4,64]{0,2,1:T(8,128)S(1)}, ...), condition=%wide.region_5.6_spmd.clone, body=%wide.region_3.5_spmd.clone.sunk | while | flops 67961344 | bytes 2957412 | solution.py:72
  123.9 10.4 all-to-all-done.1
  144.6 28.5 %while.135 = (s32[]{:T(128)}, f32[128,4,64]{0,2,1:T(8,128)}, f32[4,512,512]{2,1,0:T(8,128)}, bf16[4,512,256]{1,2,0:T(8,128)(2,1)}, bf16[128,4,64]{0,2,1:T(8,128)...) while((s32[]{:T(128)}, f32[128,4,64]{0,2,1:T(8,128)}, ...), condition=%wide.region_20.21_spmd.clone, body=%wide.region_19.20_spmd.clone.sunk | while | flops 169836544 | bytes 14422651 | solution.py:125
  178.8 73.0 %all-gather.10.cloned.1.call-done = bf16[2048,256]{1,0:T(8,128)(2,1)} async-done(((bf16[32,256]{1,0:T(8,128)(2,1)}), bf16[2048,256]{1,0:T(8,128)(2,1)}) %all-gather.10.cloned.1.call-update) | async-done | bytes 1048592 | tf_op jit(solution)/shard_map/all_gather | solution.py:166
  264.3 65.3 %all-gather.12.cloned.1.call-done = bf16[2048,256]{1,0:T(8,128)(2,1)} async-done(((bf16[32,256]{1,0:T(8,128)(2,1)}), bf16[2048,256]{1,0:T(8,128)(2,1)}) %all-gather.12.cloned.1.call-update) | async-done | bytes 1048592 | tf_op jit(solution)/shard_map/all_gather | solution.py:166
  331.9 10.4 while.131
  343.6 6.9 all-to-all-start.4
  352.9 10.4 while.132
  363.4 43.7 %all-gather.14.cloned.1.call-done = bf16[2048,256]{1,0:T(8,128)(2,1)} async-done(((bf16[32,256]{1,0:T(8,128)(2,1)}), bf16[2048,256]{1,0:T(8,128)(2,1)}) %all-gather.14.cloned.1.call-update) | async-done | bytes 1048592 | tf_op jit(solution)/shard_map/all_gather | solution.py:166
  409.4 7.0 while.133
  417.8 7.0 while.134
  428.0 28.6 %while.136 = (s32[]{:T(128)}, f32[128,4,64]{0,2,1:T(8,128)}, f32[4,512,512]{2,1,0:T(8,128)}, bf16[4,512,256]{1,2,0:T(8,128)(2,1)}, bf16[128,4,64]{0,2,1:T(8,128)...) while((s32[]{:T(128)}, f32[128,4,64]{0,2,1:T(8,128)}, ...), condition=%wide.region_23.24_spmd.clone, body=%wide.region_22.23_spmd.clone.sunk | while | flops 169836544 | bytes 14422651 | solution.py:125
  460.7 23.3 %while.137 = (s32[]{:T(128)}, f32[128,4,64]{0,2,1:T(8,128)S(1)}, f32[4,512,512]{2,1,0:T(8,128)}, bf16[4,512,256]{1,2,0:T(8,128)(2,1)}, bf16[128,4,64]{0,2,1:T(8,...) while((s32[]{:T(128)}, f32[128,4,64]{0,2,1:T(8,128)S(1)}, ...), condition=%wide.region_26.27_spmd.clone, body=%wide.region_25.26_spmd.clone.sunk | while | flops 169836544 | bytes 14422651 | solution.py:125
  488.1 16.6 %while.138 = (s32[]{:T(128)}, f32[128,4,64]{0,2,1:T(8,128)S(1)}, f32[4,512,512]{2,1,0:T(8,128)}, bf16[4,512,256]{1,2,0:T(8,128)(2,1)}, bf16[128,4,64]{0,2,1:T(8,...) while((s32[]{:T(128)}, f32[128,4,64]{0,2,1:T(8,128)S(1)}, ...), condition=%wide.region_29.30_spmd.clone, body=%wide.region_28.29_spmd.clone.sunk | while | flops 169836544 | bytes 14422651 | solution.py:125
  508.7 16.6 %while.139 = (s32[]{:T(128)}, f32[128,4,64]{0,2,1:T(8,128)S(1)}, f32[4,512,512]{2,1,0:T(8,128)}, bf16[4,512,256]{1,2,0:T(8,128)(2,1)}, bf16[128,4,64]{0,2,1:T(8,...) while((s32[]{:T(128)}, f32[128,4,64]{0,2,1:T(8,128)S(1)}, ...), condition=%wide.region_32.33_spmd.clone, body=%wide.region_31.32_spmd.clone.sunk | while | flops 169836544 | bytes 14422651 | solution.py:125
  531.0 16.8 %reduce-scatter.6.cloned.1.call-done = f32[32,512]{1,0:T(8,128)} async-done(((f32[2048,512]{1,0:T(8,128)}), f32[32,512]{1,0:T(8,128)}) %reduce-scatter.6.cloned.1.call-update) | async-done | bytes 65552 | tf_op jit(solution)/shard_map/reduce_scatter | solution.py:174
  548.5 146.1 %reduce-scatter.8.cloned.1.call-done = f32[32,512]{1,0:T(8,128)} async-done(((f32[2048,512]{1,0:T(8,128)}), f32[32,512]{1,0:T(8,128)}) %reduce-scatter.8.cloned.1.call-update) | async-done | bytes 65552 | tf_op jit(solution)/shard_map/reduce_scatter | solution.py:174
  695.4 146.1 %reduce-scatter.10.cloned.1.call-done = f32[32,512]{1,0:T(8,128)} async-done(((f32[2048,512]{1,0:T(8,128)}), f32[32,512]{1,0:T(8,128)}) %reduce-scatter.10.cloned.1.call-update) | async-done | bytes 65552 | tf_op jit(solution)/shard_map/reduce_scatter | solution.py:174
  842.3 146.0 %reduce-scatter.12.cloned.1.call-done = f32[32,512]{1,0:T(8,128)} async-done(((f32[2048,512]{1,0:T(8,128)}), f32[32,512]{1,0:T(8,128)}) %reduce-scatter.12.cloned.1.call-update) | async-done | bytes 65552 | tf_op jit(solution)/shard_map/reduce_scatter | solution.py:174
  989.0 145.9 %reduce-scatter.14.cloned.1.call-done = f32[32,512]{1,0:T(8,128)} async-done(((f32[2048,512]{1,0:T(8,128)}), f32[32,512]{1,0:T(8,128)}) %reduce-scatter.14.cloned.1.call-update) | async-done | bytes 65552 | tf_op jit(solution)/shard_map/reduce_scatter | solution.py:174
  1142.5 79.7 %all-reduce = (f32[64]{0:T(128)}, f32[64]{0:T(128)}) all-reduce(f32[64]{0:T(128)S(1)} %reduce_sum.179, f32[64]{0:T(128)S(1)} %reduce_sum.182), channel_id=1, replica_groups=mesh['img'=4,'seq'=64] {'img','seq'}, use_global_device_ids=true, to_apply=%region_42.43 | all-reduce | flops 128 | bytes 1024 | tf_op jit(solution)/shard_map/psum | solution.py:195
  (491 shorter events, 251.9 us)
Async XLA Ops:
  7.2 87.5 %all-gather.6.cloned.1.call-start = ((), (), s32[]{:S(2)}) async-start(), calls=%async_computation.10 | async-start | bytes 1064960 | tf_op jit(solution)/shard_map/all_gather | solution.py:166
  13.3 161.0 %all-gather.8.cloned.1.call-start = ((), (), s32[]{:S(2)}) async-start(), calls=%async_computation.11 | async-start | bytes 1064960 | tf_op jit(solution)/shard_map/all_gather | solution.py:166
  14.0 237.8 %all-gather.10.cloned.1.call-start = ((), (), s32[]{:S(2)}) async-start(), calls=%async_computation.12 | async-start | bytes 1064960 | tf_op jit(solution)/shard_map/all_gather | solution.py:166
  14.8 314.8 %all-gather.12.cloned.1.call-start = ((), (), s32[]{:S(2)}) async-start(), calls=%async_computation.13 | async-start | bytes 1064960 | tf_op jit(solution)/shard_map/all_gather | solution.py:166
  17.3 79.6 %all-to-all-start = ((bf16[64,32,256]{2,1,0:T(8,128)(2,1)}), bf16[64,32,256]{2,1,0:T(8,128)(2,1)S(1)}, u32[]{:S(2)}, u32[]{:S(2)}) async-start(bf16[64,32,256]{2,1,0:T(8,128)(2,1)} %stack.10), calls=%async_computation | async-start | bytes 2097152 | tf_op jit(solution)/shard_map/all_to_all | solution.py:13
  30.3 376.8 %all-gather.14.cloned.1.call-start = ((), (), s32[]{:S(2)}) async-start(), calls=%async_computation.14 | async-start | bytes 1064960 | tf_op jit(solution)/shard_map/all_gather | solution.py:166
  98.8 35.5 %all-to-all-start.1 = ((bf16[64,32,256]{2,1,0:T(8,128)(2,1)}), bf16[64,32,256]{2,1,0:T(8,128)(2,1)S(1)}, u32[]{:S(2)}, u32[]{:S(2)}) async-start(bf16[64,32,256]{2,1,0:T(8,128)(2,1)} %stack.11), calls=%async_computation.1 | async-start | bytes 2097152 | tf_op jit(solution)/shard_map/all_to_all | solution.py:13
  135.6 118.5 %all-to-all-start.2 = ((bf16[64,32,256]{2,1,0:T(8,128)(2,1)}), bf16[64,32,256]{2,1,0:T(8,128)(2,1)}, u32[]{:S(2)}, u32[]{:S(2)}) async-start(bf16[64,32,256]{2,1,0:T(8,128)(2,1)} %stack.12), calls=%async_computation.2 | async-start | bytes 2097152 | tf_op jit(solution)/shard_map/all_to_all | solution.py:13
  173.1 81.0 %copy-start.45 = (bf16[32,256]{1,0:T(8,128)(2,1)S(1)}, bf16[32,256]{1,0:T(8,128)(2,1)}, u32[]{:S(2)}) copy-start(bf16[32,256]{1,0:T(8,128)(2,1)} %get-tuple-element.1132) | copy-start | bytes 49156
  254.1 77.7 %copy-start.43 = (f32[128,4]{0,1:T(4,128)S(1)}, f32[128,4]{0,1:T(4,128)}, u32[]{:S(2)}) copy-start(f32[128,4]{0,1:T(4,128)} %custom-call.2) | copy-start | bytes 6148
  255.3 87.0 %all-to-all-start.3 = ((bf16[64,32,256]{2,1,0:T(8,128)(2,1)}), bf16[64,32,256]{2,1,0:T(8,128)(2,1)S(1)}, u32[]{:S(2)}, u32[]{:S(2)}) async-start(bf16[64,32,256]{2,1,0:T(8,128)(2,1)} %stack.13), calls=%async_computation.3 | async-start | bytes 2097152 | tf_op jit(solution)/shard_map/all_to_all | solution.py:13
  343.6 72.8 %all-to-all-start.4 = ((bf16[64,32,256]{2,1,0:T(8,128)(2,1)}), bf16[64,32,256]{2,1,0:T(8,128)(2,1)S(1)}, u32[]{:S(2)}, u32[]{:S(2)}) async-start(bf16[64,32,256]{2,1,0:T(8,128)(2,1)} %stack.14), calls=%async_computation.4 | async-start | bytes 2097152 | tf_op jit(solution)/shard_map/all_to_all | solution.py:13
  350.5 197.2 %reduce-scatter.6.cloned.1.call-start = ((), (), s32[]{:S(2)}) async-start(), calls=%async_computation.15 | async-start | bytes 4259840 | tf_op jit(solution)/shard_map/reduce_scatter | solution.py:174
  363.3 331.3 %reduce-scatter.8.cloned.1.call-start = ((), (), s32[]{:S(2)}) async-start(), calls=%async_computation.16 | async-start | bytes 4259840 | tf_op jit(solution)/shard_map/reduce_scatter | solution.py:174
  456.6 384.9 %reduce-scatter.10.cloned.1.call-start = ((), (), s32[]{:S(2)}) async-start(), calls=%async_computation.17 | async-start | bytes 4259840 | tf_op jit(solution)/shard_map/reduce_scatter | solution.py:174
  484.1 504.2 %reduce-scatter.12.cloned.1.call-start = ((), (), s32[]{:S(2)}) async-start(), calls=%async_computation.18 | async-start | bytes 4259840 | tf_op jit(solution)/shard_map/reduce_scatter | solution.py:174
  504.6 630.3 %reduce-scatter.14.cloned.1.call-start = ((), (), s32[]{:S(2)}) async-start(), calls=%async_computation.19 | async-start | bytes 4259840 | tf_op jit(solution)/shard_map/reduce_scatter | solution.py:174
  525.4 610.9 %copy-start.50 = (s32[1,128]{1,0:T(1,128)S(1)}, s32[1,128]{1,0:T(1,128)}, u32[]{:S(2)}) copy-start(s32[1,128]{1,0:T(1,128)} %param.32) | copy-start | bytes 1540
  526.3 612.3 %copy-start.5 = (f32[1,128,1280]{1,2,0:T(8,128)S(1)}, f32[1,128,1280]{1,2,0:T(8,128)}, u32[]{:S(2)}) copy-start(f32[1,128,1280]{1,2,0:T(8,128)} %copy-done.4) | copy-start | bytes 1966084
  526.3 612.3 %copy-start.38 = (f32[128,20]{0,1:T(8,128)S(1)}, f32[128,20]{0,1:T(8,128)}, u32[]{:S(2)}) copy-start(f32[128,20]{0,1:T(8,128)} %copy-done.37) | copy-start | bytes 30724
  526.3 612.3 %copy-start.49 = (f32[64]{0:T(128)S(1)}, f32[64]{0:T(128)}, u32[]{:S(2)}) copy-start(f32[64]{0:T(128)} %param.35) | copy-start | bytes 772
  528.2 612.0 %copy-start.3 = (f32[128,1280]{1,0:T(8,128)S(1)}, f32[128,1280]{1,0:T(8,128)}, u32[]{:S(2)}) copy-start(f32[128,1280]{1,0:T(8,128)} %copy-done.2) | copy-start | bytes 1966084
  528.2 612.1 %copy-start.24 = (bf16[1,128,1280]{2,1,0:T(8,128)(2,1)S(1)}, bf16[1,128,1280]{2,1,0:T(8,128)(2,1)}, u32[]{:S(2)}) copy-start(bf16[1,128,1280]{2,1,0:T(8,128)(2,1)} %param.29) | copy-start | bytes 983044
  1136.4 85.8 %copy-start.1 = (bf16[1,128,1280]{2,1,0:T(8,128)(2,1)S(1)}, bf16[1,128,1280]{2,1,0:T(8,128)(2,1)}, u32[]{:S(2)}) copy-start(bf16[1,128,1280]{2,1,0:T(8,128)(2,1)} %param.30) | copy-start | bytes 983044
  (43 other events, 586.0 us)
Sparse Core Ops, SparseCore 0:
  13.4 81.2 all-gather.5
  97.4 76.7 all-gather.7
  177.0 74.7 all-gather.9
  254.4 75.0 all-gather.11
  332.2 74.8 all-gather.13
  411.0 136.6 reduce-scatter.5
  551.9 142.6 reduce-scatter.7
  698.7 142.6 reduce-scatter.9
  845.6 142.5 reduce-scatter.11
  992.2 142.6 reduce-scatter.13
